TPU v7x, 32 devices: a whole 2x2x4 slice. The times are simulated.
32 devices in a mesh: groups: 2 (over y), hours: 4 (over z), years: 2 (over x), lines: 2 (over core).
Axes of the slice: x: 2, y: 2, z: 4, core: 2. Of those that a mesh axis runs over, the one named last changes fastest.
Arguments:
- demand: bfloat16 [8, 4, 2048], P(('groups', 'years'), 'hours'), parts along dimension 0, may hold values from 0.19921875 to 0.796875
- avail: bfloat16 [8, 4, 4096], P(('groups', 'years'), 'hours', 'lines'), parts along dimension 0, may hold values from 0.099609375 to 1
- ptdf: bfloat16 [1536, 2048], P('lines'), may hold values from -0.125 to 0.125
- line_limit: float32 [1536], P('lines'), may hold values from 0.3 to 3
- gen_cost: float32 [4096], P('lines'), may hold values from 0.2 to 5
- gen_cap: float32 [4096], P('lines'), may hold values from 0.3 to 1.5
- gen_node: int32 [4096], P('lines'), may hold values from 0 to 2047
- store_node: int32 [8192], P('lines'), may hold values from 0 to 2047
- store_power: float32 [8192], P('lines'), may hold values from 0.2 to 1
- capex: float32 [8192], P('lines'), may hold values from 0.05 to 1
- gen_state: float32 [8, 4, 4096], P(('groups', 'years'), 'hours', 'lines'), parts along dimension 0, may hold values from 0 to 0.6
- store_state: float32 [8, 4, 8192], P(('groups', 'years'), 'hours', 'lines'), parts along dimension 0, may hold values from -0.5 to 0.5
- level_upper: float32 [8, 4, 8192], P(('groups', 'years'), 'hours', 'lines'), parts along dimension 0, may hold values from 0 to 9, as said below
- level_lower: float32 [8, 4, 8192], P(('groups', 'years'), 'hours', 'lines'), parts along dimension 0, may hold values from 0 to 0.5
- flow_dual: float32 [8, 4, 1536], P(('groups', 'years'), 'hours', 'lines'), parts along dimension 0, may hold values from -3 to 3
- balance_dual: float32 [8, 4], P(('groups', 'years'), 'hours'), parts along dimension 0, may hold values from -6 to 6
- capacity: float32 [16384], P(('groups', 'lines')), parts along dimension 0, may hold values from 0.05 to 2
Outputs:
- gen_next: float32 [8, 4, 4096], P(('groups', 'years'), 'hours', 'lines'), parts along dimension 0
- store_next: float32 [8, 4, 8192], P(('groups', 'years'), 'hours', 'lines'), parts along dimension 0
- capacity_next: float32 [16384], P(('groups', 'lines')), parts along dimension 0
- balance_next: float32 [8, 4], P(('groups', 'years'), 'hours'), parts along dimension 0
- flow_next: float32 [8, 4, 1536], P(('groups', 'years'), 'hours', 'lines'), parts along dimension 0
- upper_next: float32 [8, 4, 8192], P(('groups', 'years'), 'hours', 'lines'), parts along dimension 0
- lower_next: float32 [8, 4, 8192], P(('groups', 'years'), 'hours', 'lines'), parts along dimension 0
There are 2 independent parts, one for each index of `groups`. A program takes and returns all parts, laid end to end along the dimension named above; an argument that names none is the same for every part. Nothing has to cross between parts.
Inputs may be any that keep to these rules, and one draw needn't show every extreme that they name: `level_upper`: nonnegative.
All inputs are finite; a program needn't handle non-finite values.
Results may differ from a plain program's by a relative error of at most 0.004.
Values may be sent and summed in bfloat16 or wider, within the bound.
A program may use at most 64 MiB of HBM per device.

v0:
```python
import math

import jax
import jax.numpy as jnp
from jax import lax
from jax.sharding import PartitionSpec as P

TAU = 0.1
SIGMA = 0.5
TAU_CAP = 1.0


def level_of(storage_bar, level_scale):
    inside = lax.cumsum(storage_bar, axis=1)
    totals = inside[:, -1, :]
    blocks = lax.all_gather(totals[None], "hours", axis=0, tiled=True)
    positions = lax.iota(jnp.int32, blocks.shape[0])
    weight = (positions < lax.axis_index("hours")).astype(jnp.float32)
    before = jnp.sum(blocks * weight[:, None, None], axis=0)
    return level_scale * (inside + before[:, None, :])


def dual_terms(upper, lower, level_scale):
    inside = lax.cumsum(upper - lower, axis=1, reverse=True)
    totals = inside[:, 0, :]
    local_upper = jnp.sum(upper, axis=(0, 1))
    blocks, upper_blocks = (
        lax.all_gather(totals[None], "hours", axis=0, tiled=True),
        lax.all_gather(local_upper[None], "hours", axis=0, tiled=True),
    )
    positions = lax.iota(jnp.int32, blocks.shape[0])
    weight = (positions > lax.axis_index("hours")).astype(jnp.float32)
    beyond = jnp.sum(blocks * weight[:, None, None], axis=0)
    upper_total = lax.psum(jnp.sum(upper_blocks, axis=0), "years")
    return (level_scale * (inside + beyond[:, None, :]), upper_total)


def local(
    demand,
    avail,
    ptdf,
    line_limit,
    gen_cost,
    gen_cap,
    gen_node,
    store_node,
    store_power,
    capex,
    gen_state,
    store_state,
    level_upper,
    level_lower,
    flow_dual,
    balance_dual,
    capacity,
):
    years_dev, hours_dev, nodes = demand.shape
    row_count = years_dev * hours_dev
    line_local = ptdf.shape[0]
    hours_total = hours_dev * lax.axis_size("hours")
    hour_count = years_dev * lax.axis_size("years") * hours_total
    level_scale = 1.0 / math.sqrt(hours_total)
    node_scale = 1.0 / math.sqrt(nodes)
    demand_full = demand.reshape(row_count, nodes).astype(jnp.float32)
    gen_limit = gen_cap * avail.reshape(row_count, -1).astype(jnp.float32)
    dispatch = gen_state.reshape(row_count, -1)
    upper, lower = (level_upper, level_lower)
    balance = balance_dual
    flat_dual = flow_dual.reshape(row_count, line_local)
    ptdf_all, limit_all, line_dual = (ptdf, line_limit, flat_dual)
    network = jnp.dot(line_dual.astype(jnp.bfloat16), ptdf_all, preferred_element_type=jnp.float32)
    network = lax.psum(network, "lines")
    prices = node_scale * balance + network
    dispatch_next = jnp.clip(
        dispatch - TAU * (gen_cost + jnp.take(prices, gen_node, axis=1)), 0.0, gen_limit
    )
    suffix, upper_total = dual_terms(upper, lower, level_scale)
    store_prices = jnp.take(prices, store_node, axis=1).reshape(store_state.shape)
    storage_next = jnp.clip(store_state - TAU * (suffix - store_prices), -store_power, store_power)
    capacity_next = jnp.maximum(capacity - TAU_CAP * (capex - upper_total / hour_count), 0.0)
    dispatch_bar = 2.0 * dispatch_next - dispatch
    storage_bar = 2.0 * storage_next - store_state
    capacity_bar = 2.0 * capacity_next - capacity
    empty = jnp.zeros((row_count, nodes), jnp.float32)
    partial_value = (
        empty.at[:, gen_node]
        .add(dispatch_bar)
        .at[:, store_node]
        .add(-storage_bar.reshape(row_count, -1))
    )
    inject = lax.psum(partial_value, "lines") - demand_full
    balance = balance + SIGMA * node_scale * jnp.sum(inject, axis=1).reshape(years_dev, hours_dev)
    line_flows = jnp.einsum(
        "rn,ln->rl", inject.astype(jnp.bfloat16), ptdf_all, preferred_element_type=jnp.float32
    )
    shifted = line_dual + SIGMA * line_flows
    line_dual = shifted - SIGMA * jnp.clip(shifted / SIGMA, -limit_all, limit_all)
    level = level_of(storage_bar, level_scale)
    upper = jnp.maximum(upper + SIGMA * (level - capacity_bar), 0.0)
    lower = jnp.maximum(lower - SIGMA * level, 0.0)
    gen_out = dispatch_next.reshape(years_dev, hours_dev, -1)
    flow_out = line_dual.reshape(years_dev, hours_dev, line_local)
    return (gen_out, storage_next, capacity_next, balance, flow_out, upper, lower)


def solution(mesh):
    in_specs = (
        P(("groups", "years"), "hours", None),
        P(("groups", "years"), "hours", "lines"),
        P("lines", None),
        P("lines"),
        P("lines"),
        P("lines"),
        P("lines"),
        P("lines"),
        P("lines"),
        P("lines"),
        P(("groups", "years"), "hours", "lines"),
        P(("groups", "years"), "hours", "lines"),
        P(("groups", "years"), "hours", "lines"),
        P(("groups", "years"), "hours", "lines"),
        P(("groups", "years"), "hours", "lines"),
        P(("groups", "years"), "hours"),
        P(("groups", "lines")),
    )
    out_specs = (
        P(("groups", "years"), "hours", "lines"),
        P(("groups", "years"), "hours", "lines"),
        P(("groups", "lines")),
        P(("groups", "years"), "hours"),
        P(("groups", "years"), "hours", "lines"),
        P(("groups", "years"), "hours", "lines"),
        P(("groups", "years"), "hours", "lines"),
    )
    return jax.shard_map(local, mesh=mesh, in_specs=in_specs, out_specs=out_specs, check_vma=False)
```

profile of v0, /device:TPU:0, one launch (start us, length us, event | category | flops | bytes accessed | tf_op | source)
XLA Modules:
  0.0 147.9 jit_solution(5253210586689712864)
XLA Ops:
  0.6 0.0 copy-start
  0.6 0.0 copy-start.7
  0.7 0.0 copy-start.14
  0.7 0.0 copy-start.4
  0.7 0.0 copy-start.8
  0.7 0.0 copy-start.9
  0.7 1.8 %copy-done = bf16[768,2048]{1,0:T(8,128)(2,1)S(1)} copy-done((bf16[768,2048]{1,0:T(8,128)(2,1)S(1)}, bf16[768,2048]{1,0:T(8,128)(2,1)}, u32[]{:S(2)}) %copy-start) | copy-done | bytes 3145752
  2.6 1.2 fusion.28
  3.8 3.8 %psum.21 = f32[2,2048]{1,0:T(2,128)S(1)} all-reduce(f32[2,2048]{1,0:T(2,128)S(1)} %fusion.28), channel_id=1, replica_groups=mesh['groups'=2,'hours'=4,'years'=2,'lines'=2] {'lines'}, use_global_device_ids=true, to_apply=%region_0.0 | all-reduce | flops 4096 | bytes 32768 | tf_op jit(solution)/shard_map/psum | solution.py:72
  7.6 0.1 broadcast_add_fusion
  7.7 1.4 copy.126
  9.0 0.6 compare_select_fusion.1
  9.6 8.8 %gather_fusion = f32[2048,2]{1,0:T(8,128)} fusion(f32[2,2048]{0,1:T(8,128)} %copy.126, s32[2048]{0:T(1024)S(1)} %get-tuple-element.52), kind=kCustom, calls=%fused_computation | custom fusion | bytes 40960 | tf_op jit(solution)/shard_map/jit(_take)/gather | solution.py:75
  18.4 1.6 %copy.127 = f32[2048,2]{0,1:T(2,128)S(1)} copy(f32[2048,2]{1,0:T(8,128)} %gather_fusion) | data formatting | bytes 32768 | tf_op jit(solution)/shard_map/jit(_take)/gather | solution.py:75
  20.0 0.0 copy-done.7
  20.1 0.6 copy.143
  20.7 0.6 compare_select_fusion
  21.3 15.3 %gather_fusion.1 = f32[4096,2]{1,0:T(8,128)} fusion(f32[2,2048]{0,1:T(8,128)} %copy.126, s32[4096]{0:T(1024)S(1)} %get-tuple-element.50), kind=kCustom, calls=%fused_computation.1 | custom fusion | bytes 81920 | tf_op jit(solution)/shard_map/jit(_take)/gather | solution.py:78
  36.6 2.2 %copy.133 = f32[4096,2]{0,1:T(2,128)S(1)} copy(f32[4096,2]{1,0:T(8,128)} %gather_fusion.1) | data formatting | bytes 65536 | tf_op jit(solution)/shard_map/jit(_take)/gather | solution.py:78
  38.8 0.6 compare_and_fusion
  39.6 14.8 %all-gather = f32[8,1,4096]{2,1,0:T(1,128)S(1)} all-gather(f32[2,1,4096]{2,1,0:T(1,128)S(1)} %copy.131), channel_id=2, replica_groups=mesh['groups'=2,'hours'=4,'years'=2,'lines'=2] {'hours'}, dimensions={0}, use_global_device_ids=true | all-gather | bytes 163840 | tf_op jit(solution)/shard_map/all_gather | solution.py:28
  54.3 0.3 reduce
  54.6 0.1 reshape.190
  54.7 0.1 multiply_reduce_fusion.1
  54.9 0.7 neg.12
  55.6 0.9 negate_bitcast_fusion
  56.5 0.6 copy.144
  57.2 13.1 %all-gather.1 = f32[16384]{0:T(1024)S(1)} all-gather(f32[4096]{0:T(1024)S(1)} %reduce_sum.46), channel_id=3, replica_groups=mesh['groups'=2,'hours'=4,'years'=2,'lines'=2] {'hours'}, dimensions={0}, use_global_device_ids=true | all-gather | bytes 81920 | tf_op jit(solution)/shard_map/all_gather | solution.py:29
  70.4 8.1 %psum.22 = f32[4096]{0:T(1024)S(1)} all-reduce(f32[4096]{0:T(1024)S(1)} %reduce_sum.47), channel_id=1, replica_groups=mesh['groups'=2,'hours'=4,'years'=2,'lines'=2] {'years'}, use_global_device_ids=true, to_apply=%region_4.5 | all-reduce | flops 4096 | bytes 32768 | tf_op jit(solution)/shard_map/psum | solution.py:34
  78.5 1.3 multiply_subtract_fusion.1
  79.9 0.8 fusion.18
  80.7 1.4 copy.136
  82.0 12.8 %scatter_custom_fusion = f32[2,2048]{0,1:T(8,128)} fusion(s32[2048]{0:T(1024)} %get-tuple-element.51, f32[2048,2]{1,0:T(8,128)} %copy.136, f32[]{:T(128)} %constant.19.clone.1), kind=kCustom, calls=%fused_computation.9 | custom fusion | flops 4096 | bytes 16896 | tf_op jit(solution)/shard_map/scatter-add | solution.py:87
  94.9 2.0 %copy.138 = f32[4096,2]{1,0:T(8,128)} copy(f32[4096,2]{0,1:T(2,128)S(1)} %get-tuple-element.44) | data formatting | bytes 65536 | tf_op jit(solution)/shard_map/neg | solution.py:89
  96.9 22.6 %scatter_fusion = f32[2,2048]{0,1:T(8,128)} fusion(f32[2,2048]{0,1:T(8,128)} %scatter_custom_fusion, s32[4096]{0:T(1024)} %get-tuple-element.49, f32[4096,2]{1,0:T(8,128)} %copy.138), kind=kCustom, calls=%fused_computation.3 | custom fusion | flops 8192 | bytes 114688 | tf_op jit(solution)/shard_map/scatter-add | solution.py:89
  119.5 6.9 %psum.23 = f32[2,2048]{0,1:T(8,128)} all-reduce(f32[2,2048]{0,1:T(8,128)} %scatter_fusion), channel_id=1, replica_groups=mesh['groups'=2,'hours'=4,'years'=2,'lines'=2] {'lines'}, use_global_device_ids=true, to_apply=%region_7.8 | all-reduce | flops 4096 | bytes 32768 | tf_op jit(solution)/shard_map/psum | solution.py:91
  126.4 1.1 copy.139
  127.5 1.6 %fusion.2 = f32[2]{0:T(128)S(1)} fusion(f32[2,2048]{0,1:T(8,128)} %psum.23, bf16[2,1,2048]{0,2,1:T(8,128)(2,1)} %copy.139), kind=kLoop, calls=%fused_computation.8 | loop fusion | flops 12286 | bytes 24584 | tf_op jit(solution)/shard_map/reduce_sum | solution.py:92
  129.1 0.5 bitcast_add_fusion.2
  129.7 2.3 %subtract_bitcast_fusion = f32[2,1,768]{2,0,1:T(2,128)S(1)} fusion(bf16[768,2048]{1,0:T(8,128)(2,1)S(1)} %copy-done, f32[2,2048]{0,1:T(8,128)} %psum.23, bf16[2,1,2048]{0,2,1:T(8,128)(2,1)} %copy.139, f32[2,1,768]{2,1,0:T(1,128)S(1)} %copy-done.12, f32[768]{0:T(1024)S(1)} %neg.15, f32[768]{0:T(1024)S(1)} %copy-done.11), kind=kOutput, calls=%fused_computation.55 | convolution fusion | flops 6314496 | bytes 3188736 | tf_op jit(solution)/shard_map/rn,ln->rl/dot_general | solution.py:93
  132.0 0.6 copy.145
  132.6 13.4 %all-gather.2 = f32[8,1,4096]{2,1,0:T(1,128)S(1)} all-gather(f32[2,1,4096]{2,1,0:T(1,128)S(1)} %copy.140), channel_id=4, replica_groups=mesh['groups'=2,'hours'=4,'years'=2,'lines'=2] {'hours'}, dimensions={0}, use_global_device_ids=true | all-gather | bytes 163840 | tf_op jit(solution)/shard_map/all_gather | solution.py:16
  146.0 0.3 reduce.1
  146.3 0.1 reshape.192
  146.4 0.1 multiply_reduce_fusion
  146.5 0.1 subtract_maximum_fusion
  146.6 0.6 copy.146
  147.3 0.6 copy.147
  (36 shorter events, 0.3 us)
Async XLA Ops:
  0.6 1.9 %copy-start = (bf16[768,2048]{1,0:T(8,128)(2,1)S(1)}, bf16[768,2048]{1,0:T(8,128)(2,1)}, u32[]{:S(2)}) copy-start(bf16[768,2048]{1,0:T(8,128)(2,1)} %param.19) | copy-start | bytes 9437188
  0.6 19.4 %copy-start.7 = (bf16[2,1,2048]{2,0,1:T(2,128)(2,1)S(1)}, bf16[2,1,2048]{2,0,1:T(2,128)(2,1)}, u32[]{:S(2)}) copy-start(bf16[2,1,2048]{2,0,1:T(2,128)(2,1)} %param.18) | copy-start | bytes 24580
  0.7 6.9 %copy-start.14 = (f32[2,1]{0,1:T(1,128)S(1)}, f32[2,1]{0,1:T(1,128)}, u32[]{:S(2)}) copy-start(f32[2,1]{0,1:T(1,128)} %param.32) | copy-start | bytes 28
  0.7 8.4 %copy-start.6 = (s32[2048]{0:T(1024)S(1)}, s32[2048]{0:T(1024)}, u32[]{:S(2)}) copy-start(s32[2048]{0:T(1024)} %param.23) | copy-start | bytes 24580
  0.7 19.3 %copy-start.4 = (f32[2,1,2048]{2,1,0:T(1,128)S(1)}, f32[2,1,2048]{2,1,0:T(1,128)}, u32[]{:S(2)}) copy-start(f32[2,1,2048]{2,1,0:T(1,128)} %param.27) | copy-start | bytes 49156
  0.7 19.3 %copy-start.8 = (f32[2048]{0:T(1024)S(1)}, f32[2048]{0:T(1024)}, u32[]{:S(2)}) copy-start(f32[2048]{0:T(1024)} %param.21) | copy-start | bytes 24580
  0.7 19.3 %copy-start.9 = (f32[2048]{0:T(1024)S(1)}, f32[2048]{0:T(1024)}, u32[]{:S(2)}) copy-start(f32[2048]{0:T(1024)} %param.22) | copy-start | bytes 24580
  0.7 20.0 %copy-start.5 = (s32[4096]{0:T(1024)S(1)}, s32[4096]{0:T(1024)}, u32[]{:S(2)}) copy-start(s32[4096]{0:T(1024)} %param.24) | copy-start | bytes 49156
  3.8 35.7 %copy-start.1 = (f32[2,1,4096]{2,1,0:T(1,128)S(1)}, f32[2,1,4096]{2,1,0:T(1,128)}, u32[]{:S(2)}) copy-start(f32[2,1,4096]{2,1,0:T(1,128)} %param.29) | copy-start | bytes 98308
  3.8 35.7 %copy-start.2 = (f32[2,1,4096]{2,1,0:T(1,128)S(1)}, f32[2,1,4096]{2,1,0:T(1,128)}, u32[]{:S(2)}) copy-start(f32[2,1,4096]{2,1,0:T(1,128)} %param.30) | copy-start | bytes 98308
  20.0 19.5 %copy-start.10 = (pred[2048]{0:T(1024)(128)(4,1)}, pred[2048]{0:T(1024)(128)(4,1)S(1)}, u32[]{:S(2)}) copy-start(pred[2048]{0:T(1024)(128)(4,1)S(1)} %compare_and_fusion.1) | copy-start | bytes 6148
  82.0 44.4 %copy-start.13 = (bf16[2,1,2048]{2,0,1:T(2,128)(2,1)S(1)}, bf16[2,1,2048]{2,0,1:T(2,128)(2,1)}, u32[]{:S(2)}) copy-start(bf16[2,1,2048]{2,0,1:T(2,128)(2,1)} %param.17) | copy-start | bytes 24580
  94.9 34.3 %copy-start.15 = (f32[2,1]{0,1:T(1,128)S(1)}, f32[2,1]{0,1:T(1,128)}, u32[]{:S(2)}) copy-start(f32[2,1]{0,1:T(1,128)} %param.32) | copy-start | bytes 28
  94.9 34.8 %copy-start.11 = (f32[768]{0:T(1024)S(1)}, f32[768]{0:T(1024)}, u32[]{:S(2)}) copy-start(f32[768]{0:T(1024)} %param.20) | copy-start | bytes 9220
  94.9 34.8 %copy-start.12 = (f32[2,1,768]{2,1,0:T(1,128)S(1)}, f32[2,1,768]{2,1,0:T(1,128)}, u32[]{:S(2)}) copy-start(f32[2,1,768]{2,1,0:T(1,128)} %param.31) | copy-start | bytes 18436
  129.1 17.4 %copy-start.3 = (f32[2,1,4096]{2,1,0:T(1,128)S(1)}, f32[2,1,4096]{2,1,0:T(1,128)}, u32[]{:S(2)}) copy-start(f32[2,1,4096]{2,1,0:T(1,128)} %param.30) | copy-start | bytes 98308
where the time goes:
time: 149 us; the launch traced here: 148 us
  blocking collectives  60.2 us (40%)
  other arithmetic  44.3 us (30%)
  local copies, waits for them, and re-layouts  39 us (26%)
  matrix products  3.5 us (2%)
    scatter-add x2, other arithmetic, local(): partial_value = empty.at[:, gen_node].add(dispatch_bar).at[:, store_node]...  35.4 us
    gather x2, local copies, waits for them, and re-layouts, local(): jnp.take(prices, store_node, axis=1).reshape(store_state.shape)  17.5 us
    all_gather x1, blocking collectives, dual_terms(): lax.all_gather(totals[None], 'hours', axis=0, tiled=True)  14.8 us
    all_gather x1, blocking collectives, level_of(): blocks = lax.all_gather(totals[None], 'hours', axis=0, tiled=True)  13.4 us
    all_gather x1, blocking collectives, dual_terms(): lax.all_gather(local_upper[None], 'hours', axis=0, tiled=True)  13.1 us
    gather x2, local copies, waits for them, and re-layouts, local(): jnp.take(prices, gen_node, axis=1)  10.3 us
    psum x1, blocking collectives, dual_terms(): upper_total = lax.psum(jnp.sum(upper_blocks, axis=0), 'years')  8.15 us
    psum x1, blocking collectives, local(): inject = lax.psum(partial_value, 'lines') - demand_full  6.93 us

commit v1 on v0

v1 whole, which is shorter than its diff:
```python
import functools
import math

import jax
import jax.numpy as jnp
from jax import lax
from jax.experimental import pallas as pl
from jax.experimental.pallas import tpu as pltpu
from jax.sharding import PartitionSpec as P

TAU = 0.1
SIGMA = 0.5
TAU_CAP = 1.0
LANES = 128
SPLITS = 3
LINK = jnp.float32
MESH = pl.DeviceIdType.MESH


def step_kernel(
    sizes,
    demand_h, avail_h, ptdf_h, limit_h, cost_h, cap_h, gnode_h, snode_h, power_h,
    capex_h, gen_h, store_h, upper_h, lower_h, flow_h, capacity_h, balance_s,
    gen_o, store_o, capacity_o, flow_o, upper_o, lower_o, balance_o,
    demand_v, avail_v, ptdf_v, limit_v, cost_v, cap_v, gnode_v, snode_v, power_v,
    capex_v, gen_v, store_v, upper_v, lower_v, flow_v, capacity_v,
    gen_w, store_w, capacity_w, flow_w, upper_w, lower_w,
    flow8, limit1, net_s, net_r, inj_s, inj_r, inj8, avail_d, demand_d,
    dual_s, dual_r, up_s, up_r, year_s, year_r, bar_s, bar_r, suffix_v, level_v,
    gbar_v, sbar_v, spread, onehot,
    in_sem, out_sem, net_sem, inj_sem, dual_sem, up_sem, year_sem, bar_sem,
):
    years_dev, hours_dev, hours, years, level_scale, node_scale, hour_count = sizes
    rows = years_dev * hours_dev
    me_h, me_y, me_l = lax.axis_index("hours"), lax.axis_index("years"), lax.axis_index("lines")
    nodes = ptdf_v.shape[1]
    hi_count = nodes // LANES
    line_local = ptdf_v.shape[0]
    gen_rows, store_rows = gnode_v.shape[0], snode_v.shape[0]
    link = dual_s.dtype

    order = (
        (upper_h, upper_v), (lower_h, lower_v), (snode_h, snode_v), (gnode_h, gnode_v),
        (flow_h, flow_v), (ptdf_h, ptdf_v), (store_h, store_v), (power_h, power_v),
        (gen_h, gen_v), (cost_h, cost_v), (cap_h, cap_v), (avail_h, avail_v),
        (demand_h, demand_v), (limit_h, limit_v), (capex_h, capex_v), (capacity_h, capacity_v),
    )
    loads = [pltpu.make_async_copy(s, d, in_sem.at[i]) for i, (s, d) in enumerate(order)]
    for copy in loads:
        copy.start()

    def hour_peer(k):
        return {"hours": lax.rem(me_h + k, hours)}

    def year_peer(k):
        return {"years": lax.rem(me_y + k, years)}

    partner = {"lines": 1 - me_l}
    barrier = pltpu.get_barrier_semaphore()
    peers = [partner] + [hour_peer(k) for k in range(1, hours)] + [year_peer(k) for k in range(1, years)]
    for peer in peers:
        pl.semaphore_signal(barrier, inc=1, device_id=peer, device_id_type=MESH)

    loads[0].wait()
    loads[1].wait()
    local_upper = None
    for y in range(years_dev):
        total = None
        for h in range(hours_dev):
            r = y * hours_dev + h
            diff = upper_v[r] - lower_v[r]
            total = diff if total is None else total + diff
            local_upper = upper_v[r] if local_upper is None else local_upper + upper_v[r]
        dual_s[y] = total.astype(link)
    up_s[...] = local_upper.astype(link)

    pl.semaphore_wait(barrier, len(peers))

    def remote(src, dst, sem, k, peer):
        return pltpu.make_async_remote_copy(
            src_ref=src, dst_ref=dst, send_sem=sem.at[0, k], recv_sem=sem.at[1, k],
            device_id=peer, device_id_type=MESH,
        )

    def dual_copy(k):
        return remote(dual_s, dual_r.at[k - 1], dual_sem, k - 1, hour_peer(hours - k))

    def bar_copy(k):
        return remote(bar_s, bar_r.at[k - 1], bar_sem, k - 1, hour_peer(k))

    ups = [remote(up_s, up_r.at[k - 1], up_sem, k - 1, hour_peer(k)) for k in range(1, hours)]
    year_copies = [remote(year_s, year_r.at[k - 1], year_sem, k - 1, year_peer(k)) for k in range(1, years)]
    net_copy = remote(net_s, net_r, net_sem, 0, partner)
    inj_copy = remote(inj_s, inj_r, inj_sem, 0, partner)

    for k in range(hours - 1, 0, -1):
        @pl.when(me_h >= k)
        def _(k=k):
            dual_copy(k).start()
    for copy in reversed(ups):
        copy.start()

    loads[2].wait()
    loads[3].wait()
    lane_rows = lax.broadcasted_iota(jnp.int32, (LANES, LANES), 0)

    def node_row(a):
        if a < store_rows:
            return snode_v[a : a + 1, :]
        return gnode_v[a - store_rows : a - store_rows + 1, :]

    for a in range(store_rows + gen_rows):
        low = jnp.broadcast_to(node_row(a) % LANES, (LANES, LANES))
        onehot[:, a * LANES : (a + 1) * LANES] = jnp.where(low == lane_rows, 1.0, 0.0).astype(jnp.bfloat16)

    loads[4].wait()
    flow8[...] = jnp.zeros_like(flow8)
    for r in range(rows):
        flow8[r : r + 1, :] = flow_v[r]
    dual_half = flow8[...].astype(jnp.bfloat16)
    loads[5].wait()
    net = jnp.dot(dual_half, ptdf_v[...], preferred_element_type=jnp.float32)
    net_s[...] = net[:rows]
    net_copy.start()

    for copy in loads[6:]:
        copy.wait()
    for y in range(years_dev):
        suffix_v[y] = jnp.zeros_like(suffix_v[y])
    for k in range(1, hours):
        @pl.when(me_h + k < hours)
        def _(k=k):
            dual_copy(k).wait_recv()
            for y in range(years_dev):
                suffix_v[y] = suffix_v[y] + dual_r[k - 1, y].astype(jnp.float32)
    for r in range(rows):
        for j in range(hi_count):
            piece = slice(j * LANES, (j + 1) * LANES)
            demand_d[r, j : j + 1, :] = demand_v[r : r + 1, piece].astype(jnp.float32)
        for j in range(gen_rows):
            piece = slice(j * LANES, (j + 1) * LANES)
            avail_d[r, j : j + 1, :] = avail_v[r : r + 1, piece].astype(jnp.float32)

    net_copy.wait_recv()
    prices = net_s[...] + net_r[...]

    def gather(r, node):
        price_row = prices[r : r + 1] + node_scale * balance_s[r]
        high, low = node // LANES, node % LANES
        result = jnp.zeros(node.shape, jnp.float32)
        for j in range(hi_count):
            table = jnp.broadcast_to(price_row[:, j * LANES : (j + 1) * LANES], node.shape)
            picked = jnp.take_along_axis(table, low, axis=1, mode="promise_in_bounds")
            result = jnp.where(high == j, picked, result)
        return result

    for y in range(years_dev):
        beyond = suffix_v[y]
        bar_total = jnp.zeros_like(beyond)
        for h in reversed(range(hours_dev)):
            r = y * hours_dev + h
            beyond = beyond + (upper_v[r] - lower_v[r])
            suffix = level_scale * beyond
            for b in range(0, store_rows, 8):
                part = slice(b, b + 8)
                price = gather(r, snode_v[part])
                power = power_v[part]
                new = store_v[r, part] - TAU * (suffix[part] - price)
                new = jnp.minimum(jnp.maximum(new, -power), power)
                store_w[r, part] = new
                sbar_v[r, part] = 2.0 * new - store_v[r, part]
            bar_total = bar_total + sbar_v[r]
        bar_s[y] = bar_total.astype(link)
    for k in range(hours - 1, 0, -1):
        @pl.when(me_h + k < hours)
        def _(k=k):
            bar_copy(k).start()
    outs = []

    def put(src, dst):
        copy = pltpu.make_async_copy(src, dst, out_sem.at[len(outs)])
        copy.start()
        outs.append(copy)

    put(store_w, store_o)
    for r in range(rows):
        for b in range(0, gen_rows, 8):
            part = slice(b, b + 8)
            price = gather(r, gnode_v[part])
            new = gen_v[r, part] - TAU * (cost_v[part] + price)
            new = jnp.minimum(jnp.maximum(new, 0.0), cap_v[part] * avail_d[r, part])
            gen_w[r, part] = new
            gbar_v[r, part] = 2.0 * new - gen_v[r, part]
    put(gen_w, gen_o)

    high_rows = lax.broadcasted_iota(jnp.int32, (hi_count, LANES), 0)
    for a in range(store_rows + gen_rows):
        hit = jnp.broadcast_to(node_row(a) // LANES, (hi_count, LANES)) == high_rows
        for r in range(rows):
            rest = -sbar_v[r, a : a + 1, :] if a < store_rows else gbar_v[r, a - store_rows : a - store_rows + 1, :]
            rest = jnp.where(hit, jnp.broadcast_to(rest, (hi_count, LANES)), 0.0)
            for p in range(SPLITS):
                piece = rest.astype(jnp.bfloat16)
                rest = rest - piece.astype(jnp.float32)
                base = (r * SPLITS + p) * hi_count
                spread[base : base + hi_count, a * LANES : (a + 1) * LANES] = piece
    placed = lax.dot_general(
        spread[...], onehot[...], (((1,), (1,)), ((), ())), preferred_element_type=jnp.float32
    )
    for r in range(rows):
        total = None
        for p in range(SPLITS):
            base = (r * SPLITS + p) * hi_count
            piece = placed[base : base + hi_count]
            total = piece if total is None else total + piece
        inj_s[r] = total
    inj_copy.start()

    for copy in ups:
        copy.wait_recv()
    upper_total = up_s[...].astype(jnp.float32)
    for k in range(1, hours):
        upper_total = upper_total + up_r[k - 1].astype(jnp.float32)
    year_s[...] = upper_total.astype(link)
    for copy in year_copies:
        copy.start()
    for c in range(line_local // LANES):
        limit1[:, c * LANES : (c + 1) * LANES] = limit_v[c : c + 1, :]
    inj8[...] = jnp.zeros_like(inj8)

    inj_copy.wait_recv()
    for r in range(rows):
        inject = inj_s[r] + inj_r[r] - demand_d[r]
        balance_o[r] = balance_s[r] + SIGMA * node_scale * jnp.sum(inject)
        for j in range(hi_count):
            inj8[r : r + 1, j * LANES : (j + 1) * LANES] = inject[j : j + 1]
    line_flows = lax.dot_general(
        inj8[...].astype(jnp.bfloat16), ptdf_v[...], (((1,), (1,)), ((), ())),
        preferred_element_type=jnp.float32,
    )
    shifted = flow8[...] + SIGMA * line_flows
    limit = limit1[...]
    line_next = shifted - SIGMA * jnp.minimum(jnp.maximum(shifted / SIGMA, -limit), limit)
    for r in range(rows):
        flow_w[r] = line_next[r : r + 1]
    put(flow_w, flow_o)

    for copy in year_copies:
        copy.wait_recv()
    for k in range(1, years):
        upper_total = upper_total + year_r[k - 1].astype(jnp.float32)
    capacity_next = jnp.maximum(capacity_v[...] - TAU_CAP * (capex_v[...] - upper_total / hour_count), 0.0)
    capacity_w[...] = capacity_next
    put(capacity_w, capacity_o)
    capacity_bar = 2.0 * capacity_next - capacity_v[...]

    for y in range(years_dev):
        level_v[y] = jnp.zeros_like(level_v[y])
    for k in range(1, hours):
        @pl.when(me_h >= k)
        def _(k=k):
            bar_copy(k).wait_recv()
            for y in range(years_dev):
                level_v[y] = level_v[y] + bar_r[k - 1, y].astype(jnp.float32)
    for y in range(years_dev):
        before = level_v[y]
        for h in range(hours_dev):
            r = y * hours_dev + h
            before = before + sbar_v[r]
            level = level_scale * before
            upper_w[r] = jnp.maximum(upper_v[r] + SIGMA * (level - capacity_bar), 0.0)
            lower_w[r] = jnp.maximum(lower_v[r] - SIGMA * level, 0.0)
    put(upper_w, upper_o)
    put(lower_w, lower_o)

    net_copy.wait_send()
    inj_copy.wait_send()
    for copy in ups + year_copies:
        copy.wait_send()
    for k in range(1, hours):
        @pl.when(me_h >= k)
        def _(k=k):
            dual_copy(k).wait_send()

        @pl.when(me_h + k < hours)
        def _(k=k):
            bar_copy(k).wait_send()
    for copy in outs:
        copy.wait()


def local(
    demand, avail, ptdf, line_limit, gen_cost, gen_cap, gen_node, store_node, store_power,
    capex, gen_state, store_state, level_upper, level_lower, flow_dual, balance_dual, capacity,
):
    years_dev, hours_dev, nodes = demand.shape
    rows = years_dev * hours_dev
    hours, years = lax.axis_size("hours"), lax.axis_size("years")
    hours_total = hours_dev * hours
    hour_count = years_dev * years * hours_total
    level_scale = 1.0 / math.sqrt(hours_total)
    node_scale = 1.0 / math.sqrt(nodes)
    sizes = (years_dev, hours_dev, hours, years, level_scale, node_scale, hour_count)

    def fold(x):
        return x.reshape(-1, LANES)

    def fold_rows(x):
        return x.reshape(rows, -1, LANES)

    args = (
        demand.reshape(rows, nodes), avail.reshape(rows, -1), ptdf, fold(line_limit), fold(gen_cost),
        fold(gen_cap), fold(gen_node), fold(store_node), fold(store_power), fold(capex),
        fold_rows(gen_state), fold_rows(store_state), fold_rows(level_upper), fold_rows(level_lower),
        flow_dual.reshape(rows, 1, -1), fold(capacity), balance_dual.reshape(rows),
    )
    f32 = jnp.float32
    gen_rows, store_rows = args[6].shape[0], args[7].shape[0]
    line_local, hi_count = ptdf.shape[0], nodes // LANES
    padded = max(8, -(-rows // 8) * 8)
    out_shapes = [
        (rows, gen_rows, LANES), (rows, store_rows, LANES), (store_rows, LANES),
        (rows, 1, line_local), (rows, store_rows, LANES), (rows, store_rows, LANES),
    ]
    any_spec = pl.BlockSpec(memory_space=pl.ANY)
    smem_spec = pl.BlockSpec(memory_space=pltpu.SMEM)
    block, blocks = (store_rows, LANES), (years_dev, store_rows, LANES)
    h1, y1 = max(hours - 1, 1), max(years - 1, 1)
    dma = pltpu.SemaphoreType.DMA
    scratch = [pltpu.VMEM(a.shape, a.dtype) for a in args[:16]]
    scratch += [pltpu.VMEM(s, f32) for s in out_shapes]
    scratch += [
        pltpu.VMEM((padded, line_local), f32), pltpu.VMEM((1, line_local), f32),
        pltpu.VMEM((rows, nodes), f32), pltpu.VMEM((rows, nodes), f32),
        pltpu.VMEM((rows, hi_count, LANES), f32), pltpu.VMEM((rows, hi_count, LANES), f32),
        pltpu.VMEM((padded, nodes), f32), pltpu.VMEM((rows, gen_rows, LANES), f32),
        pltpu.VMEM((rows, hi_count, LANES), f32),
        pltpu.VMEM(blocks, LINK), pltpu.VMEM((h1,) + blocks, LINK),
        pltpu.VMEM(block, LINK), pltpu.VMEM((h1,) + block, LINK),
        pltpu.VMEM(block, LINK), pltpu.VMEM((y1,) + block, LINK),
        pltpu.VMEM(blocks, LINK), pltpu.VMEM((h1,) + blocks, LINK),
        pltpu.VMEM(blocks, f32), pltpu.VMEM(blocks, f32),
        pltpu.VMEM((rows, gen_rows, LANES), f32), pltpu.VMEM((rows, store_rows, LANES), f32),
        pltpu.VMEM((rows * SPLITS * hi_count, (gen_rows + store_rows) * LANES), jnp.bfloat16),
        pltpu.VMEM((LANES, (gen_rows + store_rows) * LANES), jnp.bfloat16),
        dma((16,)), dma((6,)), dma((2, 1)), dma((2, 1)), dma((2, h1)), dma((2, h1)), dma((2, y1)), dma((2, h1)),
    ]
    results = pl.pallas_call(
        functools.partial(step_kernel, sizes),
        out_shape=[jax.ShapeDtypeStruct(s, f32) for s in out_shapes] + [jax.ShapeDtypeStruct((rows,), f32)],
        in_specs=[any_spec] * 16 + [smem_spec],
        out_specs=[any_spec] * 6 + [smem_spec],
        scratch_shapes=scratch,
        compiler_params=pltpu.CompilerParams(
            collective_id=0, has_side_effects=True, vmem_limit_bytes=56 * 1024 * 1024
        ),
    )(*args)
    gen, store, cap, flow, upper, lower, balance = results
    return (
        gen.reshape(gen_state.shape), store.reshape(store_state.shape), cap.reshape(capacity.shape),
        balance.reshape(balance_dual.shape), flow.reshape(flow_dual.shape),
        upper.reshape(level_upper.shape), lower.reshape(level_lower.shape),
    )


def solution(mesh):
    row = P(("groups", "years"), "hours", "lines")
    line = P("lines")
    in_specs = (
        P(("groups", "years"), "hours", None), row, P("lines", None), line, line, line, line, line,
        line, line, row, row, row, row, row, P(("groups", "years"), "hours"), P(("groups", "lines")),
    )
    out_specs = (row, row, P(("groups", "lines")), P(("groups", "years"), "hours"), row, row, row)
    return jax.shard_map(local, mesh=mesh, in_specs=in_specs, out_specs=out_specs, check_vma=False)
```

time: 149 us -> 26.4 us (0.18)
  blocking collectives: 60.2 us -> 0 us
  other arithmetic: 44.3 us -> 0 us
  local copies, waits for them, and re-layouts: 39 us -> 9.22 us
  Pallas kernels: 0 us -> 16.1 us
  matrix products: 3.5 us -> 0 us
    all_gather x3 -> x0, blocking collectives: 41.3 us -> none  [the longest x1 14.8 us: dual_terms(): lax.all_gather(totals[None], 'hours', axis=0, tiled=True)]
    scatter-add x2 -> x0, other arithmetic: 35.4 us -> none  [local(): partial_value = empty.at[:, gen_node].add(dispatch_bar).at[:, store_node]...]
    gather x4 -> x0, local copies, waits for them, and re-layouts: 27.9 us -> none  [the longest x2 17.5 us: local(): jnp.take(prices, store_node, axis=1).reshape(store_state.shape)]
    psum x3 -> x0, blocking collectives: 18.9 us -> none  [the longest x1 8.15 us: dual_terms(): upper_total = lax.psum(jnp.sum(upper_blocks, axis=0), 'years')]
    pallas_call x0 -> x1, Pallas kernels: none -> 16.1 us  [local(): pl.pallas_call(functools.partial(step_kernel, sizes), out_shape=[jax.Shap...]
    dot_general x2 -> x0, matrix products: 3.5 us -> none  [the longest x1 2.29 us: local(): jnp.einsum('rn,ln->rl', inject.astype(jnp.bfloat16), ptdf_all, preferred_...]
    unnamed x38 -> x7, local copies, waits for them, and re-layouts: 6.16 us -> 9.22 us
    sub x3 -> x0, other arithmetic: 2.18 us -> none  [the longest x1 1.35 us: local(): capacity_bar = 2.0 * capacity_next - capacity]
where the time goes in v1:
time: 26.4 us; the launch traced here: 25.9 us
  Pallas kernels  16.1 us (61%)
  local copies, waits for them, and re-layouts  9.22 us (35%)
  between operations  0.65 us (2%)
    pallas_call x1, Pallas kernels, local(): pl.pallas_call(functools.partial(step_kernel, sizes), out_shape=[jax.Shap...  16.1 us
    unnamed x7, local copies, waits for them, and re-layouts  9.22 us

profile of v1, /device:TPU:0, one launch (start us, length us, event | category | flops | bytes accessed | tf_op | source)
XLA Modules:
  0.0 25.9 jit_solution(15974678977940189098)
XLA Ops:
  0.6 16.1 %shard_map.216 = (f32[2,16,128]{2,1,0:T(8,128)}, f32[2,32,128]{2,1,0:T(8,128)}, f32[32,128]{1,0:T(8,128)}, f32[2,1,768]{2,1,0:T(1,128)}, f32[2,32,128]{2,1,0:T(8,128)}, /*index=5*/f32[2,32,128]{2,1,0:T(8,128)}, f32[2]{0:T(128)}) custom-call(bf16[2,2048]{1,0:T(2,128)(2,1)} %bitcast.34, bf16[2,2048]{1,0:T(2,128)(2,1)} %bitcast.35, bf16[768,2048]{1,0:T(8,128)(2,1)} %ptdf_h.1, ...), custom_call_target="tpu_custom_call" | custom-call | tf_op jit(solution)/shard_map/pallas_call | solution.py:348
  16.7 1.3 %copy.35 = f32[2,1,2048]{2,1,0:T(1,128)} copy(f32[2,1,2048]{2,1,0:T(1,128)} %bitcast.33) | data formatting | bytes 32768
  18.0 1.4 %copy.36 = f32[2,1,4096]{2,1,0:T(1,128)} copy(f32[2,1,4096]{2,1,0:T(1,128)} %bitcast.26) | data formatting | bytes 65536
  19.4 1.3 %copy.37 = f32[4096]{0:T(1024)} copy(f32[4096]{0:T(1024)} %bitcast.32) | data formatting | bytes 32768
  20.7 1.2 %copy.38 = f32[2,1]{0,1:T(1,128)} copy(f32[2,1]{0,1:T(1,128)} %bitcast.41) | data formatting | bytes 16
  21.9 1.3 %copy.39 = f32[2,1,768]{2,1,0:T(1,128)} copy(f32[2,1,768]{2,1,0:T(1,128)} %get-tuple-element.39) | data formatting | bytes 12288
  23.2 1.4 %copy.40 = f32[2,1,4096]{2,1,0:T(1,128)} copy(f32[2,1,4096]{2,1,0:T(1,128)} %bitcast.25) | data formatting | bytes 65536
  24.6 1.4 %copy.41 = f32[2,1,4096]{2,1,0:T(1,128)} copy(f32[2,1,4096]{2,1,0:T(1,128)} %bitcast.24) | data formatting | bytes 65536

commit v2 on v1

--- a/solution.py
+++ b/solution.py
@@ -13,22 +13,21 @@
 TAU_CAP = 1.0
 LANES = 128
 SPLITS = 3
-LINK = jnp.float32
+LINK = jnp.bfloat16
 MESH = pl.DeviceIdType.MESH
 
 
 def step_kernel(
     sizes,
     demand_h, avail_h, ptdf_h, limit_h, cost_h, cap_h, gnode_h, snode_h, power_h,
-    capex_h, gen_h, store_h, upper_h, lower_h, flow_h, capacity_h, balance_s,
-    gen_o, store_o, capacity_o, flow_o, upper_o, lower_o, balance_o,
+    capex_h, gen_h, store_h, upper_h, lower_h, flow_h, capacity_h, balance_h,
+    gen_w, store_w, capacity_w, flow_w, upper_w, lower_w, balance_o,
     demand_v, avail_v, ptdf_v, limit_v, cost_v, cap_v, gnode_v, snode_v, power_v,
-    capex_v, gen_v, store_v, upper_v, lower_v, flow_v, capacity_v,
-    gen_w, store_w, capacity_w, flow_w, upper_w, lower_w,
+    capex_v, gen_v, store_v, upper_v, lower_v, flow_v, capacity_v, balance_v,
     flow8, limit1, net_s, net_r, inj_s, inj_r, inj8, avail_d, demand_d,
     dual_s, dual_r, up_s, up_r, year_s, year_r, bar_s, bar_r, suffix_v, level_v,
-    gbar_v, sbar_v, spread, onehot,
-    in_sem, out_sem, net_sem, inj_sem, dual_sem, up_sem, year_sem, bar_sem,
+    gbar_v, sbar_v, price_v, spread, onehot,
+    in_sem, net_sem, inj_sem, dual_sem, up_sem, year_sem, bar_sem,
 ):
     years_dev, hours_dev, hours, years, level_scale, node_scale, hour_count = sizes
     rows = years_dev * hours_dev
@@ -44,10 +43,9 @@
         (flow_h, flow_v), (ptdf_h, ptdf_v), (store_h, store_v), (power_h, power_v),
         (gen_h, gen_v), (cost_h, cost_v), (cap_h, cap_v), (avail_h, avail_v),
         (demand_h, demand_v), (limit_h, limit_v), (capex_h, capex_v), (capacity_h, capacity_v),
+        (balance_h, balance_v),
     )
     loads = [pltpu.make_async_copy(s, d, in_sem.at[i]) for i, (s, d) in enumerate(order)]
-    for copy in loads:
-        copy.start()
 
     def hour_peer(k):
         return {"hours": lax.rem(me_h + k, hours)}
@@ -60,6 +58,8 @@
     peers = [partner] + [hour_peer(k) for k in range(1, hours)] + [year_peer(k) for k in range(1, years)]
     for peer in peers:
         pl.semaphore_signal(barrier, inc=1, device_id=peer, device_id_type=MESH)
+    for copy in loads:
+        copy.start()
 
     loads[0].wait()
     loads[1].wait()
@@ -72,7 +72,7 @@
             total = diff if total is None else total + diff
             local_upper = upper_v[r] if local_upper is None else local_upper + upper_v[r]
         dual_s[y] = total.astype(link)
-    up_s[...] = local_upper.astype(link)
+    up_s[...] = local_upper
 
     pl.semaphore_wait(barrier, len(peers))
 
@@ -97,8 +97,6 @@
         @pl.when(me_h >= k)
         def _(k=k):
             dual_copy(k).start()
-    for copy in reversed(ups):
-        copy.start()
 
     loads[2].wait()
     loads[3].wait()
@@ -122,17 +120,11 @@
     net = jnp.dot(dual_half, ptdf_v[...], preferred_element_type=jnp.float32)
     net_s[...] = net[:rows]
     net_copy.start()
+    for copy in reversed(ups):
+        copy.start()
 
     for copy in loads[6:]:
         copy.wait()
-    for y in range(years_dev):
-        suffix_v[y] = jnp.zeros_like(suffix_v[y])
-    for k in range(1, hours):
-        @pl.when(me_h + k < hours)
-        def _(k=k):
-            dual_copy(k).wait_recv()
-            for y in range(years_dev):
-                suffix_v[y] = suffix_v[y] + dual_r[k - 1, y].astype(jnp.float32)
     for r in range(rows):
         for j in range(hi_count):
             piece = slice(j * LANES, (j + 1) * LANES)
@@ -145,7 +137,7 @@
     prices = net_s[...] + net_r[...]
 
     def gather(r, node):
-        price_row = prices[r : r + 1] + node_scale * balance_s[r]
+        price_row = prices[r : r + 1] + node_scale * balance_v[:, r : r + 1]
         high, low = node // LANES, node % LANES
         result = jnp.zeros(node.shape, jnp.float32)
         for j in range(hi_count):
@@ -154,6 +146,18 @@
             result = jnp.where(high == j, picked, result)
         return result
 
+    for r in range(rows):
+        for b in range(0, store_rows, 8):
+            price_v[r, b : b + 8] = gather(r, snode_v[b : b + 8])
+
+    for y in range(years_dev):
+        suffix_v[y] = jnp.zeros_like(suffix_v[y])
+    for k in range(1, hours):
+        @pl.when(me_h + k < hours)
+        def _(k=k):
+            dual_copy(k).wait_recv()
+            for y in range(years_dev):
+                suffix_v[y] = suffix_v[y] + dual_r[k - 1, y].astype(jnp.float32)
     for y in range(years_dev):
         beyond = suffix_v[y]
         bar_total = jnp.zeros_like(beyond)
@@ -161,28 +165,18 @@
             r = y * hours_dev + h
             beyond = beyond + (upper_v[r] - lower_v[r])
             suffix = level_scale * beyond
-            for b in range(0, store_rows, 8):
-                part = slice(b, b + 8)
-                price = gather(r, snode_v[part])
-                power = power_v[part]
-                new = store_v[r, part] - TAU * (suffix[part] - price)
-                new = jnp.minimum(jnp.maximum(new, -power), power)
-                store_w[r, part] = new
-                sbar_v[r, part] = 2.0 * new - store_v[r, part]
-            bar_total = bar_total + sbar_v[r]
+            power = power_v[...]
+            new = store_v[r] - TAU * (suffix - price_v[r])
+            new = jnp.minimum(jnp.maximum(new, -power), power)
+            store_w[r] = new
+            sbar = 2.0 * new - store_v[r]
+            sbar_v[r] = sbar
+            bar_total = bar_total + sbar
         bar_s[y] = bar_total.astype(link)
     for k in range(hours - 1, 0, -1):
         @pl.when(me_h + k < hours)
         def _(k=k):
             bar_copy(k).start()
-    outs = []
-
-    def put(src, dst):
-        copy = pltpu.make_async_copy(src, dst, out_sem.at[len(outs)])
-        copy.start()
-        outs.append(copy)
-
-    put(store_w, store_o)
     for r in range(rows):
         for b in range(0, gen_rows, 8):
             part = slice(b, b + 8)
@@ -191,7 +185,6 @@
             new = jnp.minimum(jnp.maximum(new, 0.0), cap_v[part] * avail_d[r, part])
             gen_w[r, part] = new
             gbar_v[r, part] = 2.0 * new - gen_v[r, part]
-    put(gen_w, gen_o)
 
     high_rows = lax.broadcasted_iota(jnp.int32, (hi_count, LANES), 0)
     for a in range(store_rows + gen_rows):
@@ -218,10 +211,10 @@
 
     for copy in ups:
         copy.wait_recv()
-    upper_total = up_s[...].astype(jnp.float32)
+    upper_total = up_s[...]
     for k in range(1, hours):
-        upper_total = upper_total + up_r[k - 1].astype(jnp.float32)
-    year_s[...] = upper_total.astype(link)
+        upper_total = upper_total + up_r[k - 1]
+    year_s[...] = upper_total
     for copy in year_copies:
         copy.start()
     for c in range(line_local // LANES):
@@ -231,7 +224,7 @@
     inj_copy.wait_recv()
     for r in range(rows):
         inject = inj_s[r] + inj_r[r] - demand_d[r]
-        balance_o[r] = balance_s[r] + SIGMA * node_scale * jnp.sum(inject)
+        balance_o[:, r : r + 1] = balance_v[:, r : r + 1] + SIGMA * node_scale * jnp.sum(inject, keepdims=True)
         for j in range(hi_count):
             inj8[r : r + 1, j * LANES : (j + 1) * LANES] = inject[j : j + 1]
     line_flows = lax.dot_general(
@@ -243,15 +236,13 @@
     line_next = shifted - SIGMA * jnp.minimum(jnp.maximum(shifted / SIGMA, -limit), limit)
     for r in range(rows):
         flow_w[r] = line_next[r : r + 1]
-    put(flow_w, flow_o)
 
     for copy in year_copies:
         copy.wait_recv()
     for k in range(1, years):
-        upper_total = upper_total + year_r[k - 1].astype(jnp.float32)
+        upper_total = upper_total + year_r[k - 1]
     capacity_next = jnp.maximum(capacity_v[...] - TAU_CAP * (capex_v[...] - upper_total / hour_count), 0.0)
     capacity_w[...] = capacity_next
-    put(capacity_w, capacity_o)
     capacity_bar = 2.0 * capacity_next - capacity_v[...]
 
     for y in range(years_dev):
@@ -270,8 +261,6 @@
             level = level_scale * before
             upper_w[r] = jnp.maximum(upper_v[r] + SIGMA * (level - capacity_bar), 0.0)
             lower_w[r] = jnp.maximum(lower_v[r] - SIGMA * level, 0.0)
-    put(upper_w, upper_o)
-    put(lower_w, lower_o)
 
     net_copy.wait_send()
     inj_copy.wait_send()
@@ -285,7 +274,14 @@
         @pl.when(me_h + k < hours)
         def _(k=k):
             bar_copy(k).wait_send()
-    for copy in outs:
+
+
+def finish_kernel(count, *refs):
+    sources, targets, sem = refs[:count], refs[count : 2 * count], refs[2 * count]
+    copies = [pltpu.make_async_copy(s, t, sem.at[i]) for i, (s, t) in enumerate(zip(sources, targets))]
+    for copy in copies:
+        copy.start()
+    for copy in copies:
         copy.wait()
 
 
@@ -312,7 +308,7 @@
         demand.reshape(rows, nodes), avail.reshape(rows, -1), ptdf, fold(line_limit), fold(gen_cost),
         fold(gen_cap), fold(gen_node), fold(store_node), fold(store_power), fold(capex),
         fold_rows(gen_state), fold_rows(store_state), fold_rows(level_upper), fold_rows(level_lower),
-        flow_dual.reshape(rows, 1, -1), fold(capacity), balance_dual.reshape(rows),
+        flow_dual.reshape(rows, 1, -1), fold(capacity), balance_dual.reshape(1, rows),
     )
     f32 = jnp.float32
     gen_rows, store_rows = args[6].shape[0], args[7].shape[0]
@@ -323,12 +319,10 @@
         (rows, 1, line_local), (rows, store_rows, LANES), (rows, store_rows, LANES),
     ]
     any_spec = pl.BlockSpec(memory_space=pl.ANY)
-    smem_spec = pl.BlockSpec(memory_space=pltpu.SMEM)
     block, blocks = (store_rows, LANES), (years_dev, store_rows, LANES)
     h1, y1 = max(hours - 1, 1), max(years - 1, 1)
     dma = pltpu.SemaphoreType.DMA
-    scratch = [pltpu.VMEM(a.shape, a.dtype) for a in args[:16]]
-    scratch += [pltpu.VMEM(s, f32) for s in out_shapes]
+    scratch = [pltpu.VMEM(a.shape, a.dtype) for a in args]
     scratch += [
         pltpu.VMEM((padded, line_local), f32), pltpu.VMEM((1, line_local), f32),
         pltpu.VMEM((rows, nodes), f32), pltpu.VMEM((rows, nodes), f32),
@@ -336,26 +330,33 @@
         pltpu.VMEM((padded, nodes), f32), pltpu.VMEM((rows, gen_rows, LANES), f32),
         pltpu.VMEM((rows, hi_count, LANES), f32),
         pltpu.VMEM(blocks, LINK), pltpu.VMEM((h1,) + blocks, LINK),
-        pltpu.VMEM(block, LINK), pltpu.VMEM((h1,) + block, LINK),
-        pltpu.VMEM(block, LINK), pltpu.VMEM((y1,) + block, LINK),
+        pltpu.VMEM(block, f32), pltpu.VMEM((h1,) + block, f32),
+        pltpu.VMEM(block, f32), pltpu.VMEM((y1,) + block, f32),
         pltpu.VMEM(blocks, LINK), pltpu.VMEM((h1,) + blocks, LINK),
         pltpu.VMEM(blocks, f32), pltpu.VMEM(blocks, f32),
         pltpu.VMEM((rows, gen_rows, LANES), f32), pltpu.VMEM((rows, store_rows, LANES), f32),
+        pltpu.VMEM((rows, store_rows, LANES), f32),
         pltpu.VMEM((rows * SPLITS * hi_count, (gen_rows + store_rows) * LANES), jnp.bfloat16),
         pltpu.VMEM((LANES, (gen_rows + store_rows) * LANES), jnp.bfloat16),
-        dma((16,)), dma((6,)), dma((2, 1)), dma((2, 1)), dma((2, h1)), dma((2, h1)), dma((2, y1)), dma((2, h1)),
+        dma((17,)), dma((2, 1)), dma((2, 1)), dma((2, h1)), dma((2, h1)), dma((2, y1)), dma((2, h1)),
     ]
     results = pl.pallas_call(
         functools.partial(step_kernel, sizes),
-        out_shape=[jax.ShapeDtypeStruct(s, f32) for s in out_shapes] + [jax.ShapeDtypeStruct((rows,), f32)],
-        in_specs=[any_spec] * 16 + [smem_spec],
-        out_specs=[any_spec] * 6 + [smem_spec],
+        out_shape=[jax.ShapeDtypeStruct(s, f32) for s in out_shapes] + [jax.ShapeDtypeStruct((1, rows), f32)],
+        in_specs=[any_spec] * 17,
+        out_specs=[pl.BlockSpec(memory_space=pltpu.VMEM)] * 7,
         scratch_shapes=scratch,
         compiler_params=pltpu.CompilerParams(
-            collective_id=0, has_side_effects=True, vmem_limit_bytes=56 * 1024 * 1024
+            collective_id=0, has_side_effects=True, vmem_limit_bytes=62 * 1024 * 1024
         ),
     )(*args)
-    gen, store, cap, flow, upper, lower, balance = results
+    gen, store, cap, flow, upper, lower, balance = pl.pallas_call(
+        functools.partial(finish_kernel, len(results)),
+        out_shape=[jax.ShapeDtypeStruct(x.shape, f32) for x in results],
+        in_specs=[any_spec] * len(results),
+        out_specs=[any_spec] * len(results),
+        scratch_shapes=[dma((len(results),))],
+    )(*results)
     return (
         gen.reshape(gen_state.shape), store.reshape(store_state.shape), cap.reshape(capacity.shape),
         balance.reshape(balance_dual.shape), flow.reshape(flow_dual.shape),

time: 26.4 us -> 20.1 us (0.76); the launches traced: 25.9 us -> 20 us
  local copies, waits for them, and re-layouts: 9.22 us -> 0 us
  Pallas kernels: 16.1 us -> 19.3 us
    unnamed x7 -> x0, local copies, waits for them, and re-layouts: 9.22 us -> none
    pallas_call x0 -> x1, Pallas kernels: none -> 5.34 us  [local(): pl.pallas_call(functools.partial(finish_kernel, len(results)), out_shape=...]
    pallas_call x1, Pallas kernels: 16.1 us -> 14 us  [local(): pl.pallas_call(functools.partial(step_kernel, sizes), out_shape=[jax.Shap...]
where the time goes in v2:
time: 20.1 us; the launch traced here: 20 us
  Pallas kernels  19.3 us (96%)
  between operations  0.65 us (3%)
    pallas_call x1, Pallas kernels, local(): pl.pallas_call(functools.partial(step_kernel, sizes), out_shape=[jax.Shap...  14 us
    pallas_call x1, Pallas kernels, local(): pl.pallas_call(functools.partial(finish_kernel, len(results)), out_shape=...  5.34 us

profile of v2, /device:TPU:0, one launch (start us, length us, event | category | flops | bytes accessed | tf_op | source)
XLA Modules:
  0.0 20.0 jit_solution(10573576583460755565)
XLA Ops:
  0.6 14.0 %shard_map.216 = (f32[2,16,128]{2,1,0:T(8,128)}, f32[2,32,128]{2,1,0:T(8,128)}, f32[32,128]{1,0:T(8,128)}, f32[2,1,768]{2,1,0:T(1,128)}, f32[2,32,128]{2,1,0:T(8...) custom-call(bf16[2,2048]{1,0:T(2,128)(2,1)} %bitcast.29, bf16[2,2048]{1,0:T(2,128)(2,1)} %bitcast.30, ...), custom_call_target="tpu_custom_call" | custom-call | tf_op jit(solution)/shard_map/pallas_call | solution.py:343
  14.6 5.3 %shard_map.217 = (f32[2,16,128]{2,1,0:T(8,128)}, f32[2,32,128]{2,1,0:T(8,128)}, f32[32,128]{1,0:T(8,128)}, f32[2,1,768]{2,1,0:T(1,128)}, f32[2,32,128]{2,1,0:T(8...) custom-call(f32[2,16,128]{2,1,0:T(8,128)} %get-tuple-element.21.refs_0_, f32[2,32,128]{2,1,0:T(8,128)} %get-tuple-element.22.refs_1_, ...), custom_call_target="tpu_custom_call" | custom-call | tf_op jit(solution)/shard_map/pallas_call | solution.py:353

commit v3 on v2

--- a/solution.py
+++ b/solution.py
@@ -12,7 +12,7 @@
 SIGMA = 0.5
 TAU_CAP = 1.0
 LANES = 128
-SPLITS = 3
+SPLITS = 2
 LINK = jnp.bfloat16
 MESH = pl.DeviceIdType.MESH
 
@@ -26,7 +26,7 @@
     capex_v, gen_v, store_v, upper_v, lower_v, flow_v, capacity_v, balance_v,
     flow8, limit1, net_s, net_r, inj_s, inj_r, inj8, avail_d, demand_d,
     dual_s, dual_r, up_s, up_r, year_s, year_r, bar_s, bar_r, suffix_v, level_v,
-    gbar_v, sbar_v, price_v, spread, onehot,
+    gbar_v, sbar_v, price_v, spread, onehot, highhot,
     in_sem, net_sem, inj_sem, dual_sem, up_sem, year_sem, bar_sem,
 ):
     years_dev, hours_dev, hours, years, level_scale, node_scale, hour_count = sizes
@@ -72,7 +72,7 @@
             total = diff if total is None else total + diff
             local_upper = upper_v[r] if local_upper is None else local_upper + upper_v[r]
         dual_s[y] = total.astype(link)
-    up_s[...] = local_upper
+    year_s[...] = local_upper
 
     pl.semaphore_wait(barrier, len(peers))
 
@@ -97,9 +97,12 @@
         @pl.when(me_h >= k)
         def _(k=k):
             dual_copy(k).start()
+    for copy in year_copies:
+        copy.start()
 
     loads[2].wait()
     loads[3].wait()
+    high_rows = lax.broadcasted_iota(jnp.int32, (hi_count, LANES), 0)
     lane_rows = lax.broadcasted_iota(jnp.int32, (LANES, LANES), 0)
 
     def node_row(a):
@@ -110,6 +113,17 @@
     for a in range(store_rows + gen_rows):
         low = jnp.broadcast_to(node_row(a) % LANES, (LANES, LANES))
         onehot[:, a * LANES : (a + 1) * LANES] = jnp.where(low == lane_rows, 1.0, 0.0).astype(jnp.bfloat16)
+        high = jnp.broadcast_to(node_row(a) // LANES, (hi_count, LANES))
+        highhot[:, a * LANES : (a + 1) * LANES] = jnp.where(high == high_rows, 1.0, 0.0).astype(jnp.bfloat16)
+
+    for copy in year_copies:
+        copy.wait_recv()
+    block_upper = year_s[...]
+    for k in range(1, years):
+        block_upper = block_upper + year_r[k - 1]
+    up_s[...] = block_upper
+    for copy in reversed(ups):
+        copy.start()
 
     loads[4].wait()
     flow8[...] = jnp.zeros_like(flow8)
@@ -120,8 +134,6 @@
     net = jnp.dot(dual_half, ptdf_v[...], preferred_element_type=jnp.float32)
     net_s[...] = net[:rows]
     net_copy.start()
-    for copy in reversed(ups):
-        copy.start()
 
     for copy in loads[6:]:
         copy.wait()
@@ -149,6 +161,33 @@
     for r in range(rows):
         for b in range(0, store_rows, 8):
             price_v[r, b : b + 8] = gather(r, snode_v[b : b + 8])
+
+    for r in range(rows):
+        for b in range(0, gen_rows, 8):
+            part = slice(b, b + 8)
+            price = gather(r, gnode_v[part])
+            new = gen_v[r, part] - TAU * (cost_v[part] + price)
+            new = jnp.minimum(jnp.maximum(new, 0.0), cap_v[part] * avail_d[r, part])
+            gen_w[r, part] = new
+            gbar_v[r, part] = 2.0 * new - gen_v[r, part]
+
+    def place(values, sign, first, count):
+        for r in range(rows):
+            rest = sign * values[r]
+            for p in range(SPLITS):
+                piece = rest.astype(jnp.bfloat16).astype(jnp.float32)
+                rest = rest - piece
+                base = (r * SPLITS + p) * hi_count
+                for a in range(count):
+                    cols = slice((first + a) * LANES, (first + a + 1) * LANES)
+                    wide = jnp.broadcast_to(piece[a : a + 1], (hi_count, LANES)).astype(jnp.bfloat16)
+                    spread[base : base + hi_count, cols] = wide * highhot[:, cols]
+        cols = slice(first * LANES, (first + count) * LANES)
+        return lax.dot_general(
+            spread[:, cols], onehot[:, cols], (((1,), (1,)), ((), ())), preferred_element_type=jnp.float32
+        )
+
+    placed = place(gbar_v, 1.0, store_rows, gen_rows)
 
     for y in range(years_dev):
         suffix_v[y] = jnp.zeros_like(suffix_v[y])
@@ -177,29 +216,7 @@
         @pl.when(me_h + k < hours)
         def _(k=k):
             bar_copy(k).start()
-    for r in range(rows):
-        for b in range(0, gen_rows, 8):
-            part = slice(b, b + 8)
-            price = gather(r, gnode_v[part])
-            new = gen_v[r, part] - TAU * (cost_v[part] + price)
-            new = jnp.minimum(jnp.maximum(new, 0.0), cap_v[part] * avail_d[r, part])
-            gen_w[r, part] = new
-            gbar_v[r, part] = 2.0 * new - gen_v[r, part]
-
-    high_rows = lax.broadcasted_iota(jnp.int32, (hi_count, LANES), 0)
-    for a in range(store_rows + gen_rows):
-        hit = jnp.broadcast_to(node_row(a) // LANES, (hi_count, LANES)) == high_rows
-        for r in range(rows):
-            rest = -sbar_v[r, a : a + 1, :] if a < store_rows else gbar_v[r, a - store_rows : a - store_rows + 1, :]
-            rest = jnp.where(hit, jnp.broadcast_to(rest, (hi_count, LANES)), 0.0)
-            for p in range(SPLITS):
-                piece = rest.astype(jnp.bfloat16)
-                rest = rest - piece.astype(jnp.float32)
-                base = (r * SPLITS + p) * hi_count
-                spread[base : base + hi_count, a * LANES : (a + 1) * LANES] = piece
-    placed = lax.dot_general(
-        spread[...], onehot[...], (((1,), (1,)), ((), ())), preferred_element_type=jnp.float32
-    )
+    placed = placed + place(sbar_v, -1.0, 0, store_rows)
     for r in range(rows):
         total = None
         for p in range(SPLITS):
@@ -209,14 +226,6 @@
         inj_s[r] = total
     inj_copy.start()
 
-    for copy in ups:
-        copy.wait_recv()
-    upper_total = up_s[...]
-    for k in range(1, hours):
-        upper_total = upper_total + up_r[k - 1]
-    year_s[...] = upper_total
-    for copy in year_copies:
-        copy.start()
     for c in range(line_local // LANES):
         limit1[:, c * LANES : (c + 1) * LANES] = limit_v[c : c + 1, :]
     inj8[...] = jnp.zeros_like(inj8)
@@ -237,10 +246,11 @@
     for r in range(rows):
         flow_w[r] = line_next[r : r + 1]
 
-    for copy in year_copies:
+    for copy in ups:
         copy.wait_recv()
-    for k in range(1, years):
-        upper_total = upper_total + year_r[k - 1]
+    upper_total = up_s[...]
+    for k in range(1, hours):
+        upper_total = upper_total + up_r[k - 1]
     capacity_next = jnp.maximum(capacity_v[...] - TAU_CAP * (capex_v[...] - upper_total / hour_count), 0.0)
     capacity_w[...] = capacity_next
     capacity_bar = 2.0 * capacity_next - capacity_v[...]
@@ -338,25 +348,26 @@
         pltpu.VMEM((rows, store_rows, LANES), f32),
         pltpu.VMEM((rows * SPLITS * hi_count, (gen_rows + store_rows) * LANES), jnp.bfloat16),
         pltpu.VMEM((LANES, (gen_rows + store_rows) * LANES), jnp.bfloat16),
+        pltpu.VMEM((hi_count, (gen_rows + store_rows) * LANES), jnp.bfloat16),
         dma((17,)), dma((2, 1)), dma((2, 1)), dma((2, h1)), dma((2, h1)), dma((2, y1)), dma((2, h1)),
     ]
     results = pl.pallas_call(
         functools.partial(step_kernel, sizes),
-        out_shape=[jax.ShapeDtypeStruct(s, f32) for s in out_shapes] + [jax.ShapeDtypeStruct((1, rows), f32)],
+        out_shape=[pltpu.VMEM(s, f32) for s in out_shapes] + [pltpu.VMEM((1, rows), f32)],
         in_specs=[any_spec] * 17,
         out_specs=[pl.BlockSpec(memory_space=pltpu.VMEM)] * 7,
         scratch_shapes=scratch,
         compiler_params=pltpu.CompilerParams(
-            collective_id=0, has_side_effects=True, vmem_limit_bytes=62 * 1024 * 1024
+            collective_id=0, has_side_effects=True, vmem_limit_bytes=56 * 1024 * 1024
         ),
     )(*args)
     gen, store, cap, flow, upper, lower, balance = pl.pallas_call(
         functools.partial(finish_kernel, len(results)),
         out_shape=[jax.ShapeDtypeStruct(x.shape, f32) for x in results],
-        in_specs=[any_spec] * len(results),
+        in_specs=[pl.BlockSpec(memory_space=pltpu.VMEM)] * len(results),
         out_specs=[any_spec] * len(results),
         scratch_shapes=[dma((len(results),))],
-    )(*results)
+    )(*[pltpu.with_memory_space_constraint(x, pltpu.VMEM) for x in results])
     return (
         gen.reshape(gen_state.shape), store.reshape(store_state.shape), cap.reshape(capacity.shape),
         balance.reshape(balance_dual.shape), flow.reshape(flow_dual.shape),

time: 20.1 us -> 15.9 us (0.79)
  Pallas kernels: 19.3 us -> 15.1 us
    pallas_call x1, Pallas kernels: 5.34 us -> 0.72 us  [local(): pl.pallas_call(functools.partial(finish_kernel, len(results)), out_shape=...]
    pallas_call x1, Pallas kernels: 14 us -> 14.4 us  [local(): pl.pallas_call(functools.partial(step_kernel, sizes), out_shape=[pltpu.VM...]
where the time goes in v3:
time: 15.9 us; the launch traced here: 15.8 us
  Pallas kernels  15.1 us (95%)
  between operations  0.65 us (4%)
    pallas_call x1, Pallas kernels, local(): pl.pallas_call(functools.partial(step_kernel, sizes), out_shape=[pltpu.VM...  14.4 us
    pallas_call x1, Pallas kernels, local(): pl.pallas_call(functools.partial(finish_kernel, len(results)), out_shape=...  0.72 us

profile of v3, /device:TPU:0, one launch (start us, length us, event | category | flops | bytes accessed | tf_op | source)
XLA Modules:
  0.0 15.8 jit_solution(15643614738543529028)
XLA Ops:
  0.6 14.4 %shard_map.216 = (f32[2,16,128]{2,1,0:T(8,128)S(1)}, f32[2,32,128]{2,1,0:T(8,128)S(1)}, f32[32,128]{1,0:T(8,128)S(1)}, f32[2,1,768]{2,1,0:T(1,128)S(1)}, f32[2,3...) custom-call(bf16[2,2048]{1,0:T(2,128)(2,1)} %bitcast.29, bf16[2,2048]{1,0:T(2,128)(2,1)} %bitcast.30, ...), custom_call_target="tpu_custom_call" | custom-call | tf_op jit(solution)/shard_map/pallas_call | solution.py:354
  15.0 0.7 %shard_map.217 = (f32[2,16,128]{2,1,0:T(8,128)}, f32[2,32,128]{2,1,0:T(8,128)}, f32[32,128]{1,0:T(8,128)}, f32[2,1,768]{2,1,0:T(1,128)}, f32[2,32,128]{2,1,0:T(8...) custom-call(f32[2,16,128]{2,1,0:T(8,128)S(1)} %get-tuple-element.21.refs_0_, f32[2,32,128]{2,1,0:T(8,128)S(1)} %get-tuple-element.22.refs_1_, ...), custom_call_target="tpu_custom_call" | custom-call | tf_op jit(solution)/shard_map/pallas_call | solution.py:364

commit v4 on v3

--- a/solution.py
+++ b/solution.py
@@ -100,21 +100,15 @@
     for copy in year_copies:
         copy.start()
 
-    loads[2].wait()
-    loads[3].wait()
-    high_rows = lax.broadcasted_iota(jnp.int32, (hi_count, LANES), 0)
-    lane_rows = lax.broadcasted_iota(jnp.int32, (LANES, LANES), 0)
-
-    def node_row(a):
-        if a < store_rows:
-            return snode_v[a : a + 1, :]
-        return gnode_v[a - store_rows : a - store_rows + 1, :]
-
-    for a in range(store_rows + gen_rows):
-        low = jnp.broadcast_to(node_row(a) % LANES, (LANES, LANES))
-        onehot[:, a * LANES : (a + 1) * LANES] = jnp.where(low == lane_rows, 1.0, 0.0).astype(jnp.bfloat16)
-        high = jnp.broadcast_to(node_row(a) // LANES, (hi_count, LANES))
-        highhot[:, a * LANES : (a + 1) * LANES] = jnp.where(high == high_rows, 1.0, 0.0).astype(jnp.bfloat16)
+    loads[4].wait()
+    flow8[...] = jnp.zeros_like(flow8)
+    for r in range(rows):
+        flow8[r : r + 1, :] = flow_v[r]
+    dual_half = flow8[...].astype(jnp.bfloat16)
+    loads[5].wait()
+    net = jnp.dot(dual_half, ptdf_v[...], preferred_element_type=jnp.float32)
+    net_s[...] = net[:rows]
+    net_copy.start()
 
     for copy in year_copies:
         copy.wait_recv()
@@ -125,15 +119,21 @@
     for copy in reversed(ups):
         copy.start()
 
-    loads[4].wait()
-    flow8[...] = jnp.zeros_like(flow8)
-    for r in range(rows):
-        flow8[r : r + 1, :] = flow_v[r]
-    dual_half = flow8[...].astype(jnp.bfloat16)
-    loads[5].wait()
-    net = jnp.dot(dual_half, ptdf_v[...], preferred_element_type=jnp.float32)
-    net_s[...] = net[:rows]
-    net_copy.start()
+    loads[2].wait()
+    loads[3].wait()
+    high_rows = lax.broadcasted_iota(jnp.int32, (hi_count, LANES), 0)
+    lane_rows = lax.broadcasted_iota(jnp.int32, (LANES, LANES), 0)
+
+    def node_row(a):
+        if a < store_rows:
+            return snode_v[a : a + 1, :]
+        return gnode_v[a - store_rows : a - store_rows + 1, :]
+
+    for a in range(store_rows + gen_rows):
+        low = jnp.broadcast_to(node_row(a) % LANES, (LANES, LANES))
+        onehot[:, a * LANES : (a + 1) * LANES] = jnp.where(low == lane_rows, 1.0, 0.0).astype(jnp.bfloat16)
+        high = jnp.broadcast_to(node_row(a) // LANES, (hi_count, LANES))
+        highhot[:, a * LANES : (a + 1) * LANES] = jnp.where(high == high_rows, 1.0, 0.0).astype(jnp.bfloat16)
 
     for copy in loads[6:]:
         copy.wait()

time: 15.9 us -> 14.8 us (0.931)
  the two profiles are of different devices: /device:TPU:0 before, /device:TPU:1 now
where the time goes in v4:
time: 14.8 us; the launch traced here: 14.7 us
  Pallas kernels  14 us (95%)
  between operations  0.65 us (4%)
    pallas_call x1, Pallas kernels, local(): pl.pallas_call(functools.partial(step_kernel, sizes), out_shape=[pltpu.VM...  13.3 us
    pallas_call x1, Pallas kernels, local(): pl.pallas_call(functools.partial(finish_kernel, len(results)), out_shape=...  0.72 us

profile of v4, /device:TPU:1, one launch (start us, length us, event | category | flops | bytes accessed | tf_op | source)
XLA Modules:
  0.0 14.7 jit_solution(16017638154802551372)
XLA Ops:
  0.6 13.3 %shard_map.216 = (f32[2,16,128]{2,1,0:T(8,128)S(1)}, f32[2,32,128]{2,1,0:T(8,128)S(1)}, f32[32,128]{1,0:T(8,128)S(1)}, f32[2,1,768]{2,1,0:T(1,128)S(1)}, f32[2,3...) custom-call(bf16[2,2048]{1,0:T(2,128)(2,1)} %bitcast.29, bf16[2,2048]{1,0:T(2,128)(2,1)} %bitcast.30, ...), custom_call_target="tpu_custom_call" | custom-call | tf_op jit(solution)/shard_map/pallas_call | solution.py:354
  14.0 0.7 %shard_map.217 = (f32[2,16,128]{2,1,0:T(8,128)}, f32[2,32,128]{2,1,0:T(8,128)}, f32[32,128]{1,0:T(8,128)}, f32[2,1,768]{2,1,0:T(1,128)}, f32[2,32,128]{2,1,0:T(8...) custom-call(f32[2,16,128]{2,1,0:T(8,128)S(1)} %get-tuple-element.21.refs_0_, f32[2,32,128]{2,1,0:T(8,128)S(1)} %get-tuple-element.22.refs_1_, ...), custom_call_target="tpu_custom_call" | custom-call | tf_op jit(solution)/shard_map/pallas_call | solution.py:364
